TPU v7x, 512 devices: a whole 4x8x8 slice. The times are simulated.
512 devices in a mesh: gz: 32 (over z_hi, x, core), gy: 16 (over z_lo, y).
Axes of the slice: x: 4, y: 8, z: 8 (z_hi: 4, z_lo: 2; z = z_hi * 2 + z_lo), core: 2. Of those that a mesh axis runs over, the one named last changes fastest.
Arguments:
- filtered: bfloat16 [16, 256, 4096], P(None, 'gz', 'gy'), may hold values from -6 to 6
- angle_index: int32 [16], replicated, may hold values from 0 to 3599
- band_offset: int32 [16, 32], P(None, 'gz'), may hold values from 0 to 12, as said below
- band_length: int32 [16, 32], P(None, 'gz'), may hold values from 4 to 12
- foot_block: int32 [16, 64, 64], P(None, 'gy'), may hold values from 0 to 62, as said below
Outputs:
- denoised: float32 [64, 256, 4096], P('gy', 'gz')
Inputs may be any that keep to these rules, and one draw needn't show every extreme that they name: band_offset + band_length <= 16 for every projection and group. foot_block[p, y, b] is b plus a shift of -2 to 2 that depends only on p and y, clipped to the range.
All inputs are finite; a program needn't handle non-finite values.
Results may differ from a plain program's by a relative error of at most 0.0041.
Values may be sent and summed in bfloat16 or wider, within the bound.
A program may use at most 64 MiB of HBM per device.

v0:
```python
import math
import jax
import jax.numpy as jnp
from jax import lax
from jax.sharding import PartitionSpec as P

X = 4096
P_SIZE = 16
NANG = 3600
BLOCK = 64
ITERS = 2
step_length = 0.25
smooth_weight = 0.3
gradient_floor = 0.01
shift_reach = 8.0


def with_halo(cells, sides, width):
    for axis, dim in sides:
        count = lax.axis_size(axis)
        ends = count - 1
        head = lax.slice_in_dim(cells, 0, width, axis=dim)
        tail = lax.slice_in_dim(cells, cells.shape[dim] - width, cells.shape[dim], axis=dim)
        cells = jnp.concatenate(
            [
                lax.ppermute(tail, axis, [(i, (i + 1) % count) for i in range(ends)]),
                cells,
                lax.ppermute(head, axis, [((i + 1) % count, i) for i in range(ends)]),
            ],
            axis=dim,
        )
    return cells


def geometry(angle_value):
    radians = 2.0 * math.pi * angle_value.astype(jnp.float32) / NANG
    stretch = 0.5 + 0.5 * jnp.abs(jnp.cos(radians))
    spread = 1.0 + jnp.abs(jnp.sin(radians))
    return (radians, stretch, spread)


def footprint(radians, stretch, spread, row_global, rows_total, block_size):
    shifted = shift_reach * jnp.sin(radians + 2.0 * math.pi * row_global / rows_total)
    inside = jnp.arange(block_size).astype(jnp.float32) - 0.5 * (block_size - 1)
    centre = block_size + inside[None, :] * stretch + shifted[:, None]
    places = jnp.arange(2 * block_size).astype(jnp.float32) + 0.5
    weights = (
        jnp.maximum(0.0, 1.0 - jnp.abs(places[None, None, :] - centre[:, :, None]) / spread)
        / spread
    )
    return weights.astype(jnp.bfloat16)


def axial_table(offsets, lengths, depth_count):
    offset_real = offsets.astype(jnp.float32)[..., None]
    length_real = lengths.astype(jnp.float32)[..., None]
    depth_place = jnp.arange(depth_count).astype(jnp.float32) + 0.5
    centre = offset_real + depth_place * length_real / depth_count
    row_number = jnp.arange(2 * depth_count)
    row_place = row_number.astype(jnp.float32) + 0.5
    triangle = jnp.maximum(0.0, 1.0 - jnp.abs(row_place - centre[..., None]))
    inside = (row_number >= offsets[..., None, None]) & (
        row_number < (offsets + lengths)[..., None, None]
    )
    return jnp.where(inside, triangle, 0.0).astype(jnp.bfloat16)


def smooth_update(current, fidelity, row_first, depth_first, rows_total, depth_total):
    row_index = row_first + jnp.arange(current.shape[0])
    depth_index = depth_first + jnp.arange(current.shape[1])
    keep_rows = ((row_index >= 0) & (row_index < rows_total - 1)).astype(jnp.float32)[:, None, None]
    keep_depth = ((depth_index >= 0) & (depth_index < depth_total - 1)).astype(jnp.float32)[
        None, :, None
    ]
    forward_rows = (
        jnp.concatenate([current[1:] - current[:-1], jnp.zeros_like(current[:1])], 0) * keep_rows
    )
    forward_depth = (
        jnp.concatenate([current[:, 1:] - current[:, :-1], jnp.zeros_like(current[:, :1])], 1)
        * keep_depth
    )
    forward_width = jnp.concatenate(
        [current[:, :, 1:] - current[:, :, :-1], jnp.zeros_like(current[:, :, :1])], 2
    )
    magnitude = jnp.sqrt(
        forward_rows * forward_rows
        + forward_depth * forward_depth
        + forward_width * forward_width
        + gradient_floor
    )
    normal_rows = forward_rows / magnitude
    normal_depth = forward_depth / magnitude
    normal_width = forward_width / magnitude
    divergence = normal_rows - jnp.concatenate(
        [jnp.zeros_like(normal_rows[:1]), normal_rows[:-1]], 0
    )
    divergence = (
        divergence
        + normal_depth
        - jnp.concatenate([jnp.zeros_like(normal_depth[:, :1]), normal_depth[:, :-1]], 1)
    )
    divergence = (
        divergence
        + normal_width
        - jnp.concatenate([jnp.zeros_like(normal_width[:, :, :1]), normal_width[:, :, :-1]], 2)
    )
    return current + step_length * (smooth_weight * divergence - (current - fidelity))


def per_device(filtered, angle_index, band_offset, band_length, foot_block):
    depth_count = filtered.shape[1]
    row_count = foot_block.shape[1]
    extended_band = with_halo(filtered, (("gz", 1),), depth_count // 2)
    axial_weights = axial_table(band_offset[:, 0], band_length[:, 0], depth_count)
    summed_rows = jnp.einsum(
        "pzv,pvu->pzu", axial_weights, extended_band, preferred_element_type=jnp.float32
    )
    columns = lax.all_gather(summed_rows.astype(jnp.bfloat16), "gy", axis=2, tiled=True)
    column_count = columns.shape[2]
    row_base = lax.axis_index("gy") * row_count
    depth_base = lax.axis_index("gz") * depth_count
    rows_total = lax.axis_size("gy") * row_count
    depth_total = lax.axis_size("gz") * depth_count
    row_global = (row_base + jnp.arange(row_count)).astype(jnp.float32)

    def one_projection(running, inputs):
        projected, angle_value, blocks = inputs
        radians, stretch, spread = geometry(angle_value)
        weights = footprint(radians, stretch, spread, row_global, rows_total, BLOCK)
        column_tiles = projected.reshape(depth_count, column_count // BLOCK, BLOCK)
        window = jnp.concatenate([column_tiles[:, blocks], column_tiles[:, blocks + 1]], axis=-1)
        product = jnp.einsum("yiu,zybu->yzbi", weights, window, preferred_element_type=jnp.float32)
        return (running + product.reshape(running.shape), None)

    initial = jnp.zeros((row_count, depth_count, X), jnp.float32)
    summed, _unused = lax.scan(one_projection, initial, (columns, angle_index, foot_block))
    backprojection = math.pi / P_SIZE * summed
    current = backprojection
    padded_fidelity = jnp.pad(backprojection, ((1, 1), (1, 1), (0, 0)))
    for turn_index in range(ITERS):
        extended = with_halo(current, (("gz", 1), ("gy", 0)), 1)
        updated = smooth_update(
            extended, padded_fidelity, row_base - 1, depth_base - 1, rows_total, depth_total
        )
        current = updated[1:-1, 1:-1]
    return current


def solution(mesh):
    return jax.shard_map(
        per_device,
        mesh=mesh,
        in_specs=(P(None, "gz", "gy"), P(), P(None, "gz"), P(None, "gz"), P(None, "gy", None)),
        out_specs=P("gy", "gz", None),
        check_vma=False,
    )
```

profile of v0, /device:TPU:191, one launch (start us, length us, event | category | flops | bytes accessed | tf_op | source)
XLA Modules:
  0.0 272.2 jit_solution(10231032295771682402)
XLA Ops:
  7.5 7.5 %collective-permute-start = (bf16[16,4,256]{2,1,0:T(4,128)(2,1)S(1)}, bf16[16,4,256]{2,1,0:T(4,128)(2,1)S(1)}, u32[]{:S(2)}, u32[]{:S(2)}) collective-permute-start(bf16[16,4,256]{2,1,0:T(4,128)(2,1)S(1)} %get-tuple-element.140), channel_id=1, source_target_pairs={{0,16},{16,32},{32,48},{48,64},{64,80},{80,96},{96,112},{112,128},... | collective-permute-start | bytes 98312 | tf_op jit(solution)/shard_map/ppermute | solution.py:26
  15.0 1.9 collective-permute-start.1
  19.1 5.4 %collective-permute-done.1 = bf16[16,4,256]{2,1,0:T(4,128)(2,1)S(1)} collective-permute-done((bf16[16,4,256]{2,1,0:T(4,128)(2,1)S(1)}, bf16[16,4,256]{2,1,0:T(4,128)(2,1)S(1)}, u32[]{:S(2)}, u32[]{:S(2)}) %collective-permute-start.1) | collective-permute-done | bytes 32800 | tf_op jit(solution)/shard_map/ppermute | solution.py:28
  24.4 1.7 convolution_convert_fusion
  26.2 55.3 %all-gather.2.cloned.1.call-done = bf16[16,8,4096]{2,1,0:T(8,128)(2,1)} async-done(((bf16[16,8,256]{2,1,0:T(8,128)(2,1)}), bf16[16,8,4096]{2,1,0:T(8,128)(2,1)}) %all-gather.2.cloned.1.call-update) | async-done | bytes 1048592 | tf_op jit(solution)/shard_map/all_gather | solution.py:118
  81.4 113.9 %while.13 = (s32[]{:T(128)}, f32[4,8,4096]{2,1,0:T(8,128)S(1)}, bf16[16,8,4096]{2,1,0:T(8,128)(2,1)}, s32[16,4,64]{2,1,0:T(4,128)}, s32[16]{0:T(128)}, /*index=5...) while((s32[]{:T(128)}, f32[4,8,4096]{2,1,0:T(8,128)S(1)}, ...), condition=%wide.region_1.2_spmd.clone, body=%wide.region_0.1_spmd.clone.sunk | while | flops 35099164 | bytes 6183707 | solution.py:136
  88.6 1.2 dynamic_slice.32
  95.7 1.2 dynamic_slice.32
  102.8 1.2 dynamic_slice.32
  109.9 1.2 dynamic_slice.32
  117.0 1.2 dynamic_slice.32
  124.2 1.2 dynamic_slice.32
  131.3 1.2 dynamic_slice.32
  138.4 1.2 dynamic_slice.32
  145.5 1.2 dynamic_slice.32
  152.6 1.2 dynamic_slice.32
  159.8 1.2 dynamic_slice.32
  188.2 1.2 dynamic_slice.32
  195.5 15.9 %collective-permute-start.2 = (f32[4,1,4096]{2,1,0:T(1,128)S(1)}, f32[4,1,4096]{2,1,0:T(1,128)S(1)}, u32[]{:S(2)}, u32[]{:S(2)}) collective-permute-start(f32[4,1,4096]{2,1,0:T(1,128)S(1)} %get-tuple-element.138), channel_id=1, source_target_pairs={{0,16},{16,32},{32,48},{48,64},{64,80},{80,96},{96,112},{112,128},... | collective-permute-start | bytes 196616 | tf_op jit(solution)/shard_map/ppermute | solution.py:26
  211.4 1.9 collective-permute-start.3
  213.3 7.9 %collective-permute-done.3 = f32[4,1,4096]{2,1,0:T(1,128)S(1)} collective-permute-done((f32[4,1,4096]{2,1,0:T(1,128)S(1)}, f32[4,1,4096]{2,1,0:T(1,128)S(1)}, u32[]{:S(2)}, u32[]{:S(2)}) %collective-permute-start.3) | collective-permute-done | bytes 65568 | tf_op jit(solution)/shard_map/ppermute | solution.py:28
  221.3 2.9 %collective-permute-start.4 = (f32[1,10,4096]{2,1,0:T(8,128)S(1)}, f32[1,10,4096]{2,1,0:T(8,128)S(1)}, u32[]{:S(2)}, u32[]{:S(2)}) collective-permute-start(f32[1,10,4096]{2,1,0:T(8,128)S(1)} %get-tuple-element.136), channel_id=1, source_target_pairs={{0,1},{1,2},{2,3},{3,4},{4,5},{5,6},{6,7},{7,8},{8,9},{9,10},{10,1... | collective-permute-start | bytes 491528 | tf_op jit(solution)/shard_map/ppermute | solution.py:26
  224.2 2.3 collective-permute-start.5
  226.6 1.8 collective-permute-done.4
  228.4 5.1 %collective-permute-done.5 = f32[1,10,4096]{2,1,0:T(8,128)S(1)} collective-permute-done((f32[1,10,4096]{2,1,0:T(8,128)S(1)}, f32[1,10,4096]{2,1,0:T(8,128)S(1)}, u32[]{:S(2)}, u32[]{:S(2)}) %collective-permute-start.5) | collective-permute-done | bytes 163872 | tf_op jit(solution)/shard_map/ppermute | solution.py:28
  237.1 3.3 %collective-permute-start.6 = (f32[4,1,4096]{2,1,0:T(1,128)S(1)}, f32[4,1,4096]{2,1,0:T(1,128)S(1)}, u32[]{:S(2)}, u32[]{:S(2)}) collective-permute-start(f32[4,1,4096]{2,1,0:T(1,128)S(1)} %get-tuple-element.132), channel_id=1, source_target_pairs={{0,16},{16,32},{32,48},{48,64},{64,80},{80,96},{96,112},{112,128},... | collective-permute-start | bytes 196616 | tf_op jit(solution)/shard_map/ppermute | solution.py:26
  240.4 1.9 collective-permute-start.7
  242.4 7.8 %collective-permute-done.7 = f32[4,1,4096]{2,1,0:T(1,128)S(1)} collective-permute-done((f32[4,1,4096]{2,1,0:T(1,128)S(1)}, f32[4,1,4096]{2,1,0:T(1,128)S(1)}, u32[]{:S(2)}, u32[]{:S(2)}) %collective-permute-start.7) | collective-permute-done | bytes 65568 | tf_op jit(solution)/shard_map/ppermute | solution.py:28
  250.3 1.9 collective-permute-start.8
  252.2 3.4 %collective-permute-start.9 = (f32[1,10,4096]{2,1,0:T(8,128)S(1)}, f32[1,10,4096]{2,1,0:T(8,128)S(1)}, u32[]{:S(2)}, u32[]{:S(2)}) collective-permute-start(f32[1,10,4096]{2,1,0:T(8,128)S(1)} %get-tuple-element.135), channel_id=1, source_target_pairs={{1,0},{2,1},{3,2},{4,3},{5,4},{6,5},{7,6},{8,7},{9,8},{10,9},{11,1... | collective-permute-start | bytes 491528 | tf_op jit(solution)/shard_map/ppermute | solution.py:28
  255.6 1.8 collective-permute-done.8
  257.4 4.0 %collective-permute-done.9 = f32[1,10,4096]{2,1,0:T(8,128)S(1)} collective-permute-done((f32[1,10,4096]{2,1,0:T(8,128)S(1)}, f32[1,10,4096]{2,1,0:T(8,128)S(1)}, u32[]{:S(2)}, u32[]{:S(2)}) %collective-permute-start.9) | collective-permute-done | bytes 163872 | tf_op jit(solution)/shard_map/ppermute | solution.py:28
  (328 shorter events, 95.8 us)
Async XLA Ops:
  6.5 74.9 %all-gather.2.cloned.1.call-start = ((), (), s32[]{:S(2)}) async-start(), calls=%async_computation | async-start | bytes 1114112 | tf_op jit(solution)/shard_map/all_gather | solution.py:118
  7.5 11.6 %collective-permute-start = (bf16[16,4,256]{2,1,0:T(4,128)(2,1)S(1)}, bf16[16,4,256]{2,1,0:T(4,128)(2,1)S(1)}, u32[]{:S(2)}, u32[]{:S(2)}) collective-permute-start(bf16[16,4,256]{2,1,0:T(4,128)(2,1)S(1)} %get-tuple-element.140), channel_id=1, source_target_pairs={{0,16},{16,32},{32,48},{48,64},{64,80},{80,96},{96,112},{112,128},... | collective-permute-start | bytes 98312 | tf_op jit(solution)/shard_map/ppermute | solution.py:26
  15.0 9.5 %collective-permute-start.1 = (bf16[16,4,256]{2,1,0:T(4,128)(2,1)S(1)}, bf16[16,4,256]{2,1,0:T(4,128)(2,1)S(1)}, u32[]{:S(2)}, u32[]{:S(2)}) collective-permute-start(bf16[16,4,256]{2,1,0:T(4,128)(2,1)S(1)} %get-tuple-element.141), channel_id=1, source_target_pairs={{16,0},{32,16},{48,32},{64,48},{80,64},{96,80},{112,96},{128,112},... | collective-permute-start | bytes 98312 | tf_op jit(solution)/shard_map/ppermute | solution.py:28
  195.5 17.8 %collective-permute-start.2 = (f32[4,1,4096]{2,1,0:T(1,128)S(1)}, f32[4,1,4096]{2,1,0:T(1,128)S(1)}, u32[]{:S(2)}, u32[]{:S(2)}) collective-permute-start(f32[4,1,4096]{2,1,0:T(1,128)S(1)} %get-tuple-element.138), channel_id=1, source_target_pairs={{0,16},{16,32},{32,48},{48,64},{64,80},{80,96},{96,112},{112,128},... | collective-permute-start | bytes 196616 | tf_op jit(solution)/shard_map/ppermute | solution.py:26
  211.4 9.8 %collective-permute-start.3 = (f32[4,1,4096]{2,1,0:T(1,128)S(1)}, f32[4,1,4096]{2,1,0:T(1,128)S(1)}, u32[]{:S(2)}, u32[]{:S(2)}) collective-permute-start(f32[4,1,4096]{2,1,0:T(1,128)S(1)} %get-tuple-element.139), channel_id=1, source_target_pairs={{16,0},{32,16},{48,32},{64,48},{80,64},{96,80},{112,96},{128,112},... | collective-permute-start | bytes 196616 | tf_op jit(solution)/shard_map/ppermute | solution.py:28
  221.3 7.1 %collective-permute-start.4 = (f32[1,10,4096]{2,1,0:T(8,128)S(1)}, f32[1,10,4096]{2,1,0:T(8,128)S(1)}, u32[]{:S(2)}, u32[]{:S(2)}) collective-permute-start(f32[1,10,4096]{2,1,0:T(8,128)S(1)} %get-tuple-element.136), channel_id=1, source_target_pairs={{0,1},{1,2},{2,3},{3,4},{4,5},{5,6},{6,7},{7,8},{8,9},{9,10},{10,1... | collective-permute-start | bytes 491528 | tf_op jit(solution)/shard_map/ppermute | solution.py:26
  224.2 9.2 %collective-permute-start.5 = (f32[1,10,4096]{2,1,0:T(8,128)S(1)}, f32[1,10,4096]{2,1,0:T(8,128)S(1)}, u32[]{:S(2)}, u32[]{:S(2)}) collective-permute-start(f32[1,10,4096]{2,1,0:T(8,128)S(1)} %get-tuple-element.137), channel_id=1, source_target_pairs={{1,0},{2,1},{3,2},{4,3},{5,4},{6,5},{7,6},{8,7},{9,8},{10,9},{11,1... | collective-permute-start | bytes 491528 | tf_op jit(solution)/shard_map/ppermute | solution.py:28
  237.1 5.3 %collective-permute-start.6 = (f32[4,1,4096]{2,1,0:T(1,128)S(1)}, f32[4,1,4096]{2,1,0:T(1,128)S(1)}, u32[]{:S(2)}, u32[]{:S(2)}) collective-permute-start(f32[4,1,4096]{2,1,0:T(1,128)S(1)} %get-tuple-element.132), channel_id=1, source_target_pairs={{0,16},{16,32},{32,48},{48,64},{64,80},{80,96},{96,112},{112,128},... | collective-permute-start | bytes 196616 | tf_op jit(solution)/shard_map/ppermute | solution.py:26
  240.4 9.8 %collective-permute-start.7 = (f32[4,1,4096]{2,1,0:T(1,128)S(1)}, f32[4,1,4096]{2,1,0:T(1,128)S(1)}, u32[]{:S(2)}, u32[]{:S(2)}) collective-permute-start(f32[4,1,4096]{2,1,0:T(1,128)S(1)} %get-tuple-element.133), channel_id=1, source_target_pairs={{16,0},{32,16},{48,32},{64,48},{80,64},{96,80},{112,96},{128,112},... | collective-permute-start | bytes 196616 | tf_op jit(solution)/shard_map/ppermute | solution.py:28
  250.3 7.1 %collective-permute-start.8 = (f32[1,10,4096]{2,1,0:T(8,128)S(1)}, f32[1,10,4096]{2,1,0:T(8,128)S(1)}, u32[]{:S(2)}, u32[]{:S(2)}) collective-permute-start(f32[1,10,4096]{2,1,0:T(8,128)S(1)} %get-tuple-element.134), channel_id=1, source_target_pairs={{0,1},{1,2},{2,3},{3,4},{4,5},{5,6},{6,7},{7,8},{8,9},{9,10},{10,1... | collective-permute-start | bytes 491528 | tf_op jit(solution)/shard_map/ppermute | solution.py:26
  252.2 9.2 %collective-permute-start.9 = (f32[1,10,4096]{2,1,0:T(8,128)S(1)}, f32[1,10,4096]{2,1,0:T(8,128)S(1)}, u32[]{:S(2)}, u32[]{:S(2)}) collective-permute-start(f32[1,10,4096]{2,1,0:T(8,128)S(1)} %get-tuple-element.135), channel_id=1, source_target_pairs={{1,0},{2,1},{3,2},{4,3},{5,4},{6,5},{7,6},{8,7},{9,8},{10,9},{11,1... | collective-permute-start | bytes 491528 | tf_op jit(solution)/shard_map/ppermute | solution.py:28
Sparse Core Ops, SparseCore 0:
  26.3 55.1 all-gather.1
where the time goes:
time: 274 us; the launch traced here: 272 us
  waiting for transfers between devices  89 us (32%)
  local copies, waits for them, and re-layouts  77.9 us (28%)
  starting transfers between devices  43 us (16%)
  other arithmetic  25.3 us (9%)
  loops' own time  14.1 us (5%)
  between operations  13.7 us (5%)
  matrix products  9.14 us (3%)
    all_gather x1, waiting for transfers between devices, per_device(): lax.all_gather(summed_rows.astype(jnp.bfloat16), 'gy', axis=2, tiled=True)  55.3 us
    dynamic_slice x32, local copies, waits for them, and re-layouts, per_device(): lax.scan(one_projection, initial, (columns, angle_index, foot_block))  33.5 us
    ppermute x5, starting transfers between devices, with_halo(): lax.ppermute(tail, axis, [(i, (i + 1) % count) for i in range(ends)])  31.5 us
    ppermute x5, waiting for transfers between devices, with_halo(): lax.ppermute(head, axis, [((i + 1) % count, i) for i in range(ends)])  30.1 us
    gather x32, local copies, waits for them, and re-layouts, one_projection(): column_tiles[:, blocks + 1]  17.4 us
    another operation x1, loops' own time, per_device(): lax.scan(one_projection, initial, (columns, angle_index, foot_block))  14.1 us
    gather x16, local copies, waits for them, and re-layouts, one_projection(): column_tiles[:, blocks]  13.1 us
    ppermute x5, starting transfers between devices, with_halo(): lax.ppermute(head, axis, [((i + 1) % count, i) for i in range(ends)])  11.5 us
  transfers between devices with their start and end apart: 11, of which 8 were waited for; matrix products, arithmetic and copies ran while one was open for 1% of the time, Pallas kernels for 0%

commit v1 on v0

--- a/solution.py
+++ b/solution.py
@@ -13,6 +13,13 @@
 smooth_weight = 0.3
 gradient_floor = 0.01
 shift_reach = 8.0
+
+
+def all_by_exchange(value, mesh_axis, dim):
+    size = lax.axis_size(mesh_axis)
+    blocks = jnp.stack([value for _ in range(size)])
+    blocks = lax.all_to_all(blocks, mesh_axis, split_axis=0, concat_axis=0)
+    return jnp.concatenate(blocks, axis=dim)
 
 
 def with_halo(cells, sides, width):
@@ -115,7 +122,7 @@
     summed_rows = jnp.einsum(
         "pzv,pvu->pzu", axial_weights, extended_band, preferred_element_type=jnp.float32
     )
-    columns = lax.all_gather(summed_rows.astype(jnp.bfloat16), "gy", axis=2, tiled=True)
+    columns = all_by_exchange(summed_rows.astype(jnp.bfloat16), "gy", 2)
     column_count = columns.shape[2]
     row_base = lax.axis_index("gy") * row_count
     depth_base = lax.axis_index("gz") * depth_count

time: 274 us -> 200 us (0.73)
  waiting for transfers between devices: 89 us -> 54.4 us
  local copies, waits for them, and re-layouts: 77.9 us -> 56.3 us
  between operations: 13.7 us -> 0.31 us
  starting transfers between devices: 43 us -> 39.7 us
    all_gather x1 -> x0, waiting for transfers between devices: 55.3 us -> none  [per_device(): lax.all_gather(summed_rows.astype(jnp.bfloat16), 'gy', axis=2, tiled=True)]
    dynamic_slice x32, local copies, waits for them, and re-layouts: 33.5 us -> 10.6 us  [per_device(): lax.scan(one_projection, initial, (columns, angle_index, foot_block))]
    all_to_all x0 -> x1, waiting for transfers between devices: none -> 20.4 us  [all_by_exchange(): blocks = lax.all_to_all(blocks, mesh_axis, split_axis=0, concat_axis=0)]
    ppermute x5, starting transfers between devices: 31.5 us -> 21.2 us  [with_halo(): lax.ppermute(tail, axis, [(i, (i + 1) % count) for i in range(ends)])]
    all_to_all x0 -> x1, starting transfers between devices: none -> 7.28 us  [all_by_exchange(): blocks = lax.all_to_all(blocks, mesh_axis, split_axis=0, concat_axis=0)]
where the time goes in v1:
time: 200 us; the launch traced here: 199 us
  local copies, waits for them, and re-layouts  56.3 us (28%)
  waiting for transfers between devices  54.4 us (27%)
  starting transfers between devices  39.7 us (20%)
  other arithmetic  25.4 us (13%)
  loops' own time  13.9 us (7%)
  matrix products  8.51 us (4%)
    ppermute x5, waiting for transfers between devices, with_halo(): lax.ppermute(head, axis, [((i + 1) % count, i) for i in range(ends)])  30.3 us
    ppermute x5, starting transfers between devices, with_halo(): lax.ppermute(tail, axis, [(i, (i + 1) % count) for i in range(ends)])  21.2 us
    all_to_all x1, waiting for transfers between devices, all_by_exchange(): blocks = lax.all_to_all(blocks, mesh_axis, split_axis=0, concat_axis=0)  20.4 us
    gather x32, local copies, waits for them, and re-layouts, one_projection(): column_tiles[:, blocks + 1]  17.4 us
    another operation x1, loops' own time, per_device(): lax.scan(one_projection, initial, (columns, angle_index, foot_block))  13.9 us
    gather x16, local copies, waits for them, and re-layouts, one_projection(): column_tiles[:, blocks]  13.1 us
    ppermute x5, starting transfers between devices, with_halo(): lax.ppermute(head, axis, [((i + 1) % count, i) for i in range(ends)])  11.3 us
    select_n x16, other arithmetic, one_projection(): column_tiles[:, blocks]  11 us
  transfers between devices with their start and end apart: 11, of which 8 were waited for; matrix products, arithmetic and copies ran while one was open for 1% of the time, Pallas kernels for 0%

profile of v1, /device:TPU:191, one launch (start us, length us, event | category | flops | bytes accessed | tf_op | source)
XLA Modules:
  0.0 198.5 jit_solution(4540691804645319273)
XLA Ops:
  0.0 0.9 fusion.43
  0.9 7.5 %collective-permute-start = (bf16[16,4,256]{2,1,0:T(4,128)(2,1)S(1)}, bf16[16,4,256]{2,1,0:T(4,128)(2,1)S(1)}, u32[]{:S(2)}, u32[]{:S(2)}) collective-permute-start(bf16[16,4,256]{2,1,0:T(4,128)(2,1)S(1)} %get-tuple-element.140), channel_id=1, source_target_pairs={{0,16},{16,32},{32,48},{48,64},{64,80},{80,96},{96,112},{112,128},... | collective-permute-start | bytes 98312 | tf_op jit(solution)/shard_map/ppermute | solution.py:33
  8.4 1.9 collective-permute-start.1
  12.6 5.4 %collective-permute-done.1 = bf16[16,4,256]{2,1,0:T(4,128)(2,1)S(1)} collective-permute-done((bf16[16,4,256]{2,1,0:T(4,128)(2,1)S(1)}, bf16[16,4,256]{2,1,0:T(4,128)(2,1)S(1)}, u32[]{:S(2)}, u32[]{:S(2)}) %collective-permute-start.1) | collective-permute-done | bytes 32800 | tf_op jit(solution)/shard_map/ppermute | solution.py:35
  17.9 1.0 convolution_convert_fusion
  19.0 1.1 stack.2
  20.1 7.3 %all-to-all-start = ((bf16[16,16,8,256]{3,2,1,0:T(8,128)(2,1)}), bf16[16,16,8,256]{3,2,1,0:T(8,128)(2,1)S(1)}, u32[]{:S(2)}, u32[]{:S(2)}) async-start(bf16[16,16,8,256]{3,2,1,0:T(8,128)(2,1)} %stack.2), calls=%async_computation | async-start | bytes 2097152 | tf_op jit(solution)/shard_map/all_to_all | solution.py:21
  27.4 20.4 %all-to-all-done = bf16[16,16,8,256]{3,2,1,0:T(8,128)(2,1)S(1)} async-done(((bf16[16,16,8,256]{3,2,1,0:T(8,128)(2,1)}), bf16[16,16,8,256]{3,2,1,0:T(8,128)(2,1)S(1)}, u32[]{:S(2)}, u32[]{:S(2)}) %all-to-all-start) | async-done | bytes 1048608 | tf_op jit(solution)/shard_map/all_to_all | solution.py:21
  47.9 90.8 %while.13 = (s32[]{:T(128)}, f32[4,8,4096]{2,1,0:T(8,128)S(1)}, bf16[16,8,4096]{2,1,0:T(8,128)(2,1)S(1)}, s32[16,4,64]{2,1,0:T(4,128)}, s32[16]{0:T(128)S(1)}, /...) while((s32[]{:T(128)}, f32[4,8,4096]{2,1,0:T(8,128)S(1)}, ...), condition=%wide.region_1.2_spmd.clone, body=%wide.region_0.1_spmd.clone.sunk | while | flops 35099164 | bytes 6183707 | solution.py:143
  56.3 0.8 gather_fusion.1
  67.7 0.8 gather_fusion.1
  101.8 0.8 gather_fusion.1
  113.1 0.8 gather_fusion.1
  124.5 0.8 gather_fusion.1
  138.9 5.4 %collective-permute-start.2 = (f32[4,1,4096]{2,1,0:T(1,128)S(1)}, f32[4,1,4096]{2,1,0:T(1,128)S(1)}, u32[]{:S(2)}, u32[]{:S(2)}) collective-permute-start(f32[4,1,4096]{2,1,0:T(1,128)S(1)} %get-tuple-element.138), channel_id=1, source_target_pairs={{0,16},{16,32},{32,48},{48,64},{64,80},{80,96},{96,112},{112,128},... | collective-permute-start | bytes 196616 | tf_op jit(solution)/shard_map/ppermute | solution.py:33
  144.3 1.9 collective-permute-start.3
  146.2 7.9 %collective-permute-done.3 = f32[4,1,4096]{2,1,0:T(1,128)S(1)} collective-permute-done((f32[4,1,4096]{2,1,0:T(1,128)S(1)}, f32[4,1,4096]{2,1,0:T(1,128)S(1)}, u32[]{:S(2)}, u32[]{:S(2)}) %collective-permute-start.3) | collective-permute-done | bytes 65568 | tf_op jit(solution)/shard_map/ppermute | solution.py:35
  154.2 2.7 %collective-permute-start.4 = (f32[1,10,4096]{2,1,0:T(8,128)S(1)}, f32[1,10,4096]{2,1,0:T(8,128)S(1)}, u32[]{:S(2)}, u32[]{:S(2)}) collective-permute-start(f32[1,10,4096]{2,1,0:T(8,128)S(1)} %get-tuple-element.136), channel_id=1, source_target_pairs={{0,1},{1,2},{2,3},{3,4},{4,5},{5,6},{6,7},{7,8},{8,9},{9,10},{10,1... | collective-permute-start | bytes 491528 | tf_op jit(solution)/shard_map/ppermute | solution.py:33
  156.9 2.6 %collective-permute-start.5 = (f32[1,10,4096]{2,1,0:T(8,128)S(1)}, f32[1,10,4096]{2,1,0:T(8,128)S(1)}, u32[]{:S(2)}, u32[]{:S(2)}) collective-permute-start(f32[1,10,4096]{2,1,0:T(8,128)S(1)} %get-tuple-element.137), channel_id=1, source_target_pairs={{1,0},{2,1},{3,2},{4,3},{5,4},{6,5},{7,6},{8,7},{9,8},{10,9},{11,1... | collective-permute-start | bytes 491528 | tf_op jit(solution)/shard_map/ppermute | solution.py:35
  159.5 1.8 collective-permute-done.4
  161.3 4.8 %collective-permute-done.5 = f32[1,10,4096]{2,1,0:T(8,128)S(1)} collective-permute-done((f32[1,10,4096]{2,1,0:T(8,128)S(1)}, f32[1,10,4096]{2,1,0:T(8,128)S(1)}, u32[]{:S(2)}, u32[]{:S(2)}) %collective-permute-start.5) | collective-permute-done | bytes 163872 | tf_op jit(solution)/shard_map/ppermute | solution.py:35
  167.2 1.1 fusion.19
  168.4 1.2 multiply_add_fusion.1
  169.7 3.3 %collective-permute-start.6 = (f32[4,1,4096]{2,1,0:T(1,128)S(1)}, f32[4,1,4096]{2,1,0:T(1,128)S(1)}, u32[]{:S(2)}, u32[]{:S(2)}) collective-permute-start(f32[4,1,4096]{2,1,0:T(1,128)S(1)} %get-tuple-element.132), channel_id=1, source_target_pairs={{0,16},{16,32},{32,48},{48,64},{64,80},{80,96},{96,112},{112,128},... | collective-permute-start | bytes 196616 | tf_op jit(solution)/shard_map/ppermute | solution.py:33
  173.0 1.9 collective-permute-start.7
  175.0 7.8 %collective-permute-done.7 = f32[4,1,4096]{2,1,0:T(1,128)S(1)} collective-permute-done((f32[4,1,4096]{2,1,0:T(1,128)S(1)}, f32[4,1,4096]{2,1,0:T(1,128)S(1)}, u32[]{:S(2)}, u32[]{:S(2)}) %collective-permute-start.7) | collective-permute-done | bytes 65568 | tf_op jit(solution)/shard_map/ppermute | solution.py:35
  182.9 2.4 %collective-permute-start.8 = (f32[1,10,4096]{2,1,0:T(8,128)S(1)}, f32[1,10,4096]{2,1,0:T(8,128)S(1)}, u32[]{:S(2)}, u32[]{:S(2)}) collective-permute-start(f32[1,10,4096]{2,1,0:T(8,128)S(1)} %get-tuple-element.134), channel_id=1, source_target_pairs={{0,1},{1,2},{2,3},{3,4},{4,5},{5,6},{6,7},{7,8},{8,9},{9,10},{10,1... | collective-permute-start | bytes 491528 | tf_op jit(solution)/shard_map/ppermute | solution.py:33
  185.3 2.9 %collective-permute-start.9 = (f32[1,10,4096]{2,1,0:T(8,128)S(1)}, f32[1,10,4096]{2,1,0:T(8,128)S(1)}, u32[]{:S(2)}, u32[]{:S(2)}) collective-permute-start(f32[1,10,4096]{2,1,0:T(8,128)S(1)} %get-tuple-element.135), channel_id=1, source_target_pairs={{1,0},{2,1},{3,2},{4,3},{5,4},{6,5},{7,6},{8,7},{9,8},{10,9},{11,1... | collective-permute-start | bytes 491528 | tf_op jit(solution)/shard_map/ppermute | solution.py:35
  188.2 1.8 collective-permute-done.8
  190.0 4.5 %collective-permute-done.9 = f32[1,10,4096]{2,1,0:T(8,128)S(1)} collective-permute-done((f32[1,10,4096]{2,1,0:T(8,128)S(1)}, f32[1,10,4096]{2,1,0:T(8,128)S(1)}, u32[]{:S(2)}, u32[]{:S(2)}) %collective-permute-start.9) | collective-permute-done | bytes 163872 | tf_op jit(solution)/shard_map/ppermute | solution.py:35
  195.7 1.1 fusion.20
  197.3 1.2 fusion.25
  (331 shorter events, 78.4 us)
Async XLA Ops:
  0.9 11.6 %collective-permute-start = (bf16[16,4,256]{2,1,0:T(4,128)(2,1)S(1)}, bf16[16,4,256]{2,1,0:T(4,128)(2,1)S(1)}, u32[]{:S(2)}, u32[]{:S(2)}) collective-permute-start(bf16[16,4,256]{2,1,0:T(4,128)(2,1)S(1)} %get-tuple-element.140), channel_id=1, source_target_pairs={{0,16},{16,32},{32,48},{48,64},{64,80},{80,96},{96,112},{112,128},... | collective-permute-start | bytes 98312 | tf_op jit(solution)/shard_map/ppermute | solution.py:33
  8.4 9.5 %collective-permute-start.1 = (bf16[16,4,256]{2,1,0:T(4,128)(2,1)S(1)}, bf16[16,4,256]{2,1,0:T(4,128)(2,1)S(1)}, u32[]{:S(2)}, u32[]{:S(2)}) collective-permute-start(bf16[16,4,256]{2,1,0:T(4,128)(2,1)S(1)} %get-tuple-element.141), channel_id=1, source_target_pairs={{16,0},{32,16},{48,32},{64,48},{80,64},{96,80},{112,96},{128,112},... | collective-permute-start | bytes 98312 | tf_op jit(solution)/shard_map/ppermute | solution.py:35
  20.1 27.7 %all-to-all-start = ((bf16[16,16,8,256]{3,2,1,0:T(8,128)(2,1)}), bf16[16,16,8,256]{3,2,1,0:T(8,128)(2,1)S(1)}, u32[]{:S(2)}, u32[]{:S(2)}) async-start(bf16[16,16,8,256]{3,2,1,0:T(8,128)(2,1)} %stack.2), calls=%async_computation | async-start | bytes 2097152 | tf_op jit(solution)/shard_map/all_to_all | solution.py:21
  27.3 20.6 %copy-start = (s32[16]{0:T(128)S(1)}, s32[16]{0:T(128)}, u32[]{:S(2)}) copy-start(s32[16]{0:T(128)} %param.8) | copy-start | bytes 196
  138.9 7.3 %collective-permute-start.2 = (f32[4,1,4096]{2,1,0:T(1,128)S(1)}, f32[4,1,4096]{2,1,0:T(1,128)S(1)}, u32[]{:S(2)}, u32[]{:S(2)}) collective-permute-start(f32[4,1,4096]{2,1,0:T(1,128)S(1)} %get-tuple-element.138), channel_id=1, source_target_pairs={{0,16},{16,32},{32,48},{48,64},{64,80},{80,96},{96,112},{112,128},... | collective-permute-start | bytes 196616 | tf_op jit(solution)/shard_map/ppermute | solution.py:33
  144.3 9.8 %collective-permute-start.3 = (f32[4,1,4096]{2,1,0:T(1,128)S(1)}, f32[4,1,4096]{2,1,0:T(1,128)S(1)}, u32[]{:S(2)}, u32[]{:S(2)}) collective-permute-start(f32[4,1,4096]{2,1,0:T(1,128)S(1)} %get-tuple-element.139), channel_id=1, source_target_pairs={{16,0},{32,16},{48,32},{64,48},{80,64},{96,80},{112,96},{128,112},... | collective-permute-start | bytes 196616 | tf_op jit(solution)/shard_map/ppermute | solution.py:35
  154.2 7.1 %collective-permute-start.4 = (f32[1,10,4096]{2,1,0:T(8,128)S(1)}, f32[1,10,4096]{2,1,0:T(8,128)S(1)}, u32[]{:S(2)}, u32[]{:S(2)}) collective-permute-start(f32[1,10,4096]{2,1,0:T(8,128)S(1)} %get-tuple-element.136), channel_id=1, source_target_pairs={{0,1},{1,2},{2,3},{3,4},{4,5},{5,6},{6,7},{7,8},{8,9},{9,10},{10,1... | collective-permute-start | bytes 491528 | tf_op jit(solution)/shard_map/ppermute | solution.py:33
  156.9 9.2 %collective-permute-start.5 = (f32[1,10,4096]{2,1,0:T(8,128)S(1)}, f32[1,10,4096]{2,1,0:T(8,128)S(1)}, u32[]{:S(2)}, u32[]{:S(2)}) collective-permute-start(f32[1,10,4096]{2,1,0:T(8,128)S(1)} %get-tuple-element.137), channel_id=1, source_target_pairs={{1,0},{2,1},{3,2},{4,3},{5,4},{6,5},{7,6},{8,7},{9,8},{10,9},{11,1... | collective-permute-start | bytes 491528 | tf_op jit(solution)/shard_map/ppermute | solution.py:35
  169.7 5.3 %collective-permute-start.6 = (f32[4,1,4096]{2,1,0:T(1,128)S(1)}, f32[4,1,4096]{2,1,0:T(1,128)S(1)}, u32[]{:S(2)}, u32[]{:S(2)}) collective-permute-start(f32[4,1,4096]{2,1,0:T(1,128)S(1)} %get-tuple-element.132), channel_id=1, source_target_pairs={{0,16},{16,32},{32,48},{48,64},{64,80},{80,96},{96,112},{112,128},... | collective-permute-start | bytes 196616 | tf_op jit(solution)/shard_map/ppermute | solution.py:33
  173.0 9.8 %collective-permute-start.7 = (f32[4,1,4096]{2,1,0:T(1,128)S(1)}, f32[4,1,4096]{2,1,0:T(1,128)S(1)}, u32[]{:S(2)}, u32[]{:S(2)}) collective-permute-start(f32[4,1,4096]{2,1,0:T(1,128)S(1)} %get-tuple-element.133), channel_id=1, source_target_pairs={{16,0},{32,16},{48,32},{64,48},{80,64},{96,80},{112,96},{128,112},... | collective-permute-start | bytes 196616 | tf_op jit(solution)/shard_map/ppermute | solution.py:35
  182.9 7.1 %collective-permute-start.8 = (f32[1,10,4096]{2,1,0:T(8,128)S(1)}, f32[1,10,4096]{2,1,0:T(8,128)S(1)}, u32[]{:S(2)}, u32[]{:S(2)}) collective-permute-start(f32[1,10,4096]{2,1,0:T(8,128)S(1)} %get-tuple-element.134), channel_id=1, source_target_pairs={{0,1},{1,2},{2,3},{3,4},{4,5},{5,6},{6,7},{7,8},{8,9},{9,10},{10,1... | collective-permute-start | bytes 491528 | tf_op jit(solution)/shard_map/ppermute | solution.py:33
  185.3 9.2 %collective-permute-start.9 = (f32[1,10,4096]{2,1,0:T(8,128)S(1)}, f32[1,10,4096]{2,1,0:T(8,128)S(1)}, u32[]{:S(2)}, u32[]{:S(2)}) collective-permute-start(f32[1,10,4096]{2,1,0:T(8,128)S(1)} %get-tuple-element.135), channel_id=1, source_target_pairs={{1,0},{2,1},{3,2},{4,3},{5,4},{6,5},{7,6},{8,7},{9,8},{10,9},{11,1... | collective-permute-start | bytes 491528 | tf_op jit(solution)/shard_map/ppermute | solution.py:35
